TPU v7x, 32 devices: a whole 2x2x4 slice. The times are simulated.
32 devices in a mesh: grp: 2 (over x), seq: 8 (over z, y), mdl: 2 (over core).
Axes of the slice: x: 2, y: 2, z: 4, core: 2. Of those that a mesh axis runs over, the one named last changes fastest.
Arguments:
- signal: float32 [8, 128, 8192], P('grp', 'mdl', 'seq'), parts along dimension 0, may hold values from -6 to 6
- lengths: int32 [8], P('grp'), parts along dimension 0, may hold values from 1 to 64, 160 in all
- chan_weight: bfloat16 [128, 128, 16], P('mdl'), may hold values from -0.5 to 0.5
- up_weight: bfloat16 [4, 2048, 4096], P(None, 'seq', 'mdl'), may hold values from -0.125 to 0.125
- down_weight: bfloat16 [4, 2048, 4096], P(None, 'seq', 'mdl'), may hold values from -0.09375 to 0.09375
Outputs:
- features: bfloat16 [8, 64, 2048], P(('grp', 'mdl'), 'seq'), parts along dimension 0
There are 2 independent parts, one for each index of `grp`. A program takes and returns all parts, laid end to end along the dimension named above; an argument that names none is the same for every part. Nothing has to cross between parts.
Inputs may be any that keep to these rules, and one draw needn't show every extreme that they name: `lengths`: live windows of each recording; one recording is live for all 64, and all recordings together have (320) // 2.
All inputs are finite; a program needn't handle non-finite values.
Results may differ from a plain program's by a relative error of at most 0.014.
Values may be sent and summed in bfloat16 or wider, within the bound.
A program may use at most 128 MiB of HBM per device.

v0:
```python
import math
import jax
import jax.numpy as jnp
from jax import lax
from jax.sharding import PartitionSpec as P

HOP = 128
EPSILON = 1e-06


def shifted(x, axis, by):
    size = lax.axis_size(axis)
    pairs = [(i, i + by) for i in range(size) if 0 <= i + by < size]
    return lax.ppermute(x, axis, pairs)


def spectral_table(half_span):
    full_span = 2 * half_span
    row_index = jnp.arange(full_span, dtype=jnp.int32)
    col_index = jnp.arange(half_span, dtype=jnp.int32)
    phases = row_index[:, None] * col_index[None, :] % full_span
    angles = phases.astype(jnp.float32) * (2.0 * math.pi / full_span)
    window_taper = 0.5 - 0.5 * jnp.cos(row_index.astype(jnp.float32) * (2.0 * math.pi / full_span))
    weighting = window_taper * (1.0 / math.sqrt(full_span))
    joined = jnp.concatenate([jnp.cos(angles), -jnp.sin(angles)], axis=1) * weighting[:, None]
    return jnp.concatenate([joined[:half_span], joined[half_span:]], axis=1)


def log_power(spectrum):
    half_span = spectrum.shape[-1] // 2
    real_part = spectrum[..., :half_span]
    imag_part = spectrum[..., half_span:]
    return jnp.log1p(real_part * real_part + imag_part * imag_part).astype(jnp.bfloat16)


def project_down(hidden, own_down):
    return lax.dot_general(
        hidden, own_down, (((1,), (1,)), ((), ())), preferred_element_type=jnp.float32
    )


def apply_layer(state, up_rows, down_rows, width):
    values = state.astype(jnp.float32)
    squares = lax.psum(jnp.sum(values * values, axis=1, keepdims=True), "seq")
    partial = jnp.dot(state, up_rows, preferred_element_type=jnp.float32).astype(jnp.bfloat16)
    summed = lax.psum_scatter(partial, "seq", scatter_dimension=1, tiled=True)
    scale = lax.rsqrt(squares * (1.0 / width) + EPSILON)
    hidden = jax.nn.gelu(summed.astype(jnp.float32) * scale).astype(jnp.bfloat16)
    hidden = lax.all_gather(hidden, "seq", axis=1, tiled=True)
    added = lax.psum(project_down(hidden, down_rows), "mdl")
    return (values + added).astype(jnp.bfloat16)


def body(signal, lengths, chan_weight, up_weight, down_weight):
    streams, channels, samples = signal.shape
    frames = samples // HOP
    dft_table = spectral_table(HOP)
    boundary = shifted(signal[:, :, :HOP], "seq", -1)
    local_part = jnp.dot(
        signal.reshape(streams, channels, frames, HOP), dft_table, precision=lax.Precision.HIGHEST
    )
    edge_part = jnp.dot(boundary, dft_table[:, 2 * HOP :], precision=lax.Precision.HIGHEST)
    following = jnp.concatenate([local_part[:, :, 1:, 2 * HOP :], edge_part[:, :, None, :]], axis=2)
    spectrum = local_part[..., : 2 * HOP] + following
    logpower = log_power(spectrum)
    embedded = jnp.einsum(
        "scfb,cbe->sfce", logpower, chan_weight, preferred_element_type=jnp.float32
    )
    embedded = embedded.reshape(streams, frames, channels * chan_weight.shape[2])
    frame_index = lax.axis_index("seq") * frames + jnp.arange(frames, dtype=jnp.int32)
    live_mask = frame_index[None, :] < lengths[:, None]
    tokens = jnp.where(live_mask[:, :, None], embedded, 0.0).astype(jnp.bfloat16)
    rows = lax.all_gather(tokens.reshape(streams * frames, -1), "mdl", axis=1, tiled=True)
    state = lax.all_to_all(rows, "seq", split_axis=1, concat_axis=0, tiled=True)
    width = rows.shape[1]
    for layer in range(up_weight.shape[0]):
        state = apply_layer(state, up_weight[layer], down_weight[layer], width)
    rows = lax.all_to_all(state, "seq", split_axis=0, concat_axis=1, tiled=True)
    full_rows = rows.reshape(streams, frames, width)
    half_streams = streams // lax.axis_size("mdl")
    return lax.dynamic_slice_in_dim(
        full_rows, lax.axis_index("mdl") * half_streams, half_streams, 0
    )


def solution(mesh):
    return jax.shard_map(
        body,
        mesh=mesh,
        in_specs=(
            P("grp", "mdl", "seq"),
            P("grp"),
            P("mdl", None, None),
            P(None, "seq", "mdl"),
            P(None, "seq", "mdl"),
        ),
        out_specs=P(("grp", "mdl"), "seq", None),
        check_vma=False,
    )
```

profile of v0, /device:TPU:0, one launch (start us, length us, event | category | flops | bytes accessed | tf_op | source)
XLA Modules:
  0.0 576.4 jit_solution(18243975974515709880)
XLA Ops:
  9.5 4.7 convolution_bitcast_fusion
  14.3 1.9 copy-done.1
  17.1 1.9 slice_add_fusion
  20.9 2.0 all_gather.15
  22.9 15.4 %all_to_all.35 = bf16[32,8,256]{2,0,1:T(8,128)(2,1)S(1)} all-to-all(bf16[32,8,256]{2,0,1:T(8,128)(2,1)S(1)} %bitcast.87), channel_id=1, replica_groups=mesh['grp'=2,'seq'=8,'mdl'=2] {'seq'}, dimensions={1} | all-to-all | bytes 262144 | tf_op jit(solution)/shard_map/all_to_all | solution.py:74
  38.4 2.7 convolution_convert_fusion.3
  41.3 18.6 %psum.56 = f32[256,1]{0,1:T(1,128)S(1)} all-reduce(f32[256,1]{0,1:T(1,128)S(1)} %broadcast_in_dim.36), channel_id=1, replica_groups=mesh['grp'=2,'seq'=8,'mdl'=2] {'seq'}, use_global_device_ids=true, to_apply=%region_2.3 | all-reduce | flops 256 | bytes 2048 | tf_op jit(solution)/shard_map/psum | solution.py:44
  59.9 43.4 %reduce-scatter.5.cloned.1.call-done = bf16[256,256]{1,0:T(8,128)(2,1)} async-done(((bf16[256,2048]{1,0:T(8,128)(2,1)}), bf16[256,256]{1,0:T(8,128)(2,1)}) %reduce-scatter.5.cloned.1.call-update) | async-done | bytes 131088 | tf_op jit(solution)/shard_map/reduce_scatter | solution.py:46
  103.2 1.7 fusion.39
  105.0 39.1 %all-gather.5.cloned.1.call-done = bf16[256,2048]{1,0:T(8,128)(2,1)} async-done(((bf16[256,256]{1,0:T(8,128)(2,1)}), bf16[256,2048]{1,0:T(8,128)(2,1)}) %all-gather.5.cloned.1.call-update) | async-done | bytes 1048592 | tf_op jit(solution)/shard_map/all_gather | solution.py:49
  144.1 2.7 fusion.14
  146.9 17.3 %all-reduce.5.cloned.1.call-done = f32[256,256]{1,0:T(8,128)} async-done(((f32[256,256]{1,0:T(8,128)}), f32[256,256]{1,0:T(8,128)}) %all-reduce.5.cloned.1.call-update) | async-done | bytes 262160 | tf_op jit(solution)/shard_map/psum | solution.py:50
  165.2 2.7 convolution_convert_fusion.2
  168.0 21.7 %psum.58 = f32[256,1]{0,1:T(1,128)S(1)} all-reduce(f32[256,1]{0,1:T(1,128)S(1)} %bitcast.88), channel_id=1, replica_groups=mesh['grp'=2,'seq'=8,'mdl'=2] {'seq'}, use_global_device_ids=true, to_apply=%region_6.7 | all-reduce | flops 256 | bytes 2048 | tf_op jit(solution)/shard_map/psum | solution.py:44
  189.7 43.6 %reduce-scatter.7.cloned.1.call-done = bf16[256,256]{1,0:T(8,128)(2,1)} async-done(((bf16[256,2048]{1,0:T(8,128)(2,1)}), bf16[256,256]{1,0:T(8,128)(2,1)}) %reduce-scatter.7.cloned.1.call-update) | async-done | bytes 131088 | tf_op jit(solution)/shard_map/reduce_scatter | solution.py:46
  235.1 38.8 %all-gather.7.cloned.1.call-done = bf16[256,2048]{1,0:T(8,128)(2,1)} async-done(((bf16[256,256]{1,0:T(8,128)(2,1)}), bf16[256,2048]{1,0:T(8,128)(2,1)}) %all-gather.7.cloned.1.call-update) | async-done | bytes 1048592 | tf_op jit(solution)/shard_map/all_gather | solution.py:49
  273.9 2.7 fusion.11
  276.7 17.3 %all-reduce.7.cloned.1.call-done = f32[256,256]{1,0:T(8,128)} async-done(((f32[256,256]{1,0:T(8,128)}), f32[256,256]{1,0:T(8,128)}) %all-reduce.7.cloned.1.call-update) | async-done | bytes 262160 | tf_op jit(solution)/shard_map/psum | solution.py:50
  295.0 2.7 convolution_convert_fusion.1
  297.8 21.7 %psum.60 = f32[256,1]{0,1:T(1,128)S(1)} all-reduce(f32[256,1]{0,1:T(1,128)S(1)} %bitcast.89), channel_id=1, replica_groups=mesh['grp'=2,'seq'=8,'mdl'=2] {'seq'}, use_global_device_ids=true, to_apply=%region_10.11 | all-reduce | flops 256 | bytes 2048 | tf_op jit(solution)/shard_map/psum | solution.py:44
  319.5 43.6 %reduce-scatter.9.cloned.1.call-done = bf16[256,256]{1,0:T(8,128)(2,1)} async-done(((bf16[256,2048]{1,0:T(8,128)(2,1)}), bf16[256,256]{1,0:T(8,128)(2,1)}) %reduce-scatter.9.cloned.1.call-update) | async-done | bytes 131088 | tf_op jit(solution)/shard_map/reduce_scatter | solution.py:46
  364.9 39.0 %all-gather.9.cloned.1.call-done = bf16[256,2048]{1,0:T(8,128)(2,1)} async-done(((bf16[256,256]{1,0:T(8,128)(2,1)}), bf16[256,2048]{1,0:T(8,128)(2,1)}) %all-gather.9.cloned.1.call-update) | async-done | bytes 1048592 | tf_op jit(solution)/shard_map/all_gather | solution.py:49
  403.9 2.7 fusion.8
  406.7 17.3 %all-reduce.9.cloned.1.call-done = f32[256,256]{1,0:T(8,128)} async-done(((f32[256,256]{1,0:T(8,128)}), f32[256,256]{1,0:T(8,128)}) %all-reduce.9.cloned.1.call-update) | async-done | bytes 262160 | tf_op jit(solution)/shard_map/psum | solution.py:50
  425.0 2.7 convolution_convert_fusion
  427.7 21.7 %psum.62 = f32[256,1]{0,1:T(1,128)S(1)} all-reduce(f32[256,1]{0,1:T(1,128)S(1)} %bitcast.90), channel_id=1, replica_groups=mesh['grp'=2,'seq'=8,'mdl'=2] {'seq'}, use_global_device_ids=true, to_apply=%region_14.15 | all-reduce | flops 256 | bytes 2048 | tf_op jit(solution)/shard_map/psum | solution.py:44
  449.4 43.6 %reduce-scatter.11.cloned.1.call-done = bf16[256,256]{1,0:T(8,128)(2,1)} async-done(((bf16[256,2048]{1,0:T(8,128)(2,1)}), bf16[256,256]{1,0:T(8,128)(2,1)}) %reduce-scatter.11.cloned.1.call-update) | async-done | bytes 131088 | tf_op jit(solution)/shard_map/reduce_scatter | solution.py:46
  494.8 39.0 %all-gather.11.cloned.1.call-done = bf16[256,2048]{1,0:T(8,128)(2,1)} async-done(((bf16[256,256]{1,0:T(8,128)(2,1)}), bf16[256,2048]{1,0:T(8,128)(2,1)}) %all-gather.11.cloned.1.call-update) | async-done | bytes 1048592 | tf_op jit(solution)/shard_map/all_gather | solution.py:49
  533.8 2.7 fusion.5
  536.6 17.3 %all-reduce.11.cloned.1.call-done = f32[256,256]{1,0:T(8,128)} async-done(((f32[256,256]{1,0:T(8,128)}), f32[256,256]{1,0:T(8,128)}) %all-reduce.11.cloned.1.call-update) | async-done | bytes 262160 | tf_op jit(solution)/shard_map/psum | solution.py:50
  555.5 5.8 %all-to-all-start.1 = ((bf16[8,32,256]{2,1,0:T(8,128)(2,1)}), bf16[8,32,256]{2,1,0:T(8,128)(2,1)S(1)}, u32[]{:S(2)}, u32[]{:S(2)}) async-start(bf16[8,32,256]{2,1,0:T(8,128)(2,1)} %bitcast.27), calls=%async_computation.5 | async-start | bytes 262144 | tf_op jit(solution)/shard_map/all_to_all | solution.py:78
  561.3 7.4 %all-to-all-done.1 = bf16[8,32,256]{2,1,0:T(8,128)(2,1)S(1)} async-done(((bf16[8,32,256]{2,1,0:T(8,128)(2,1)}), bf16[8,32,256]{2,1,0:T(8,128)(2,1)S(1)}, u32[]{:S(2)}, u32[]{:S(2)}) %all-to-all-start.1) | async-done | bytes 131104 | tf_op jit(solution)/shard_map/all_to_all | solution.py:78
  (66 shorter events, 17.4 us)
Async XLA Ops:
  6.5 12.9 %copy-start = (bf16[64,128,16]{1,2,0:T(8,128)(2,1)S(1)}, bf16[64,128,16]{1,2,0:T(8,128)(2,1)}, u32[]{:S(2)}) copy-start(bf16[64,128,16]{1,2,0:T(8,128)(2,1)} %param.7) | copy-start | bytes 786436
  6.5 96.7 %reduce-scatter.5.cloned.1.call-start = ((), (), s32[]{:S(2)}) async-start(), calls=%async_computation.6 | async-start | bytes 1179648 | tf_op jit(solution)/shard_map/reduce_scatter | solution.py:46
  7.5 9.2 %collective-permute-start = (f32[4,64,128]{2,1,0:T(8,128)S(1)}, f32[4,64,128]{2,1,0:T(8,128)S(1)}, u32[]{:S(2)}, u32[]{:S(2)}) collective-permute-start(f32[4,64,128]{2,1,0:T(8,128)S(1)} %slice.49), channel_id=1, source_target_pairs={{2,0},{4,2},{6,4},{8,6},{10,8},{12,10},{14,12},{3,1},{5,3},{7,5},{... | collective-permute-start | bytes 393224 | tf_op jit(solution)/shard_map/ppermute | solution.py:14
  9.5 7.0 %copy-start.2 = (s32[4]{0:T(128)S(1)}, s32[4]{0:T(128)}, u32[]{:S(2)}) copy-start(s32[4]{0:T(128)} %param.6) | copy-start | bytes 52
  14.3 1.9 copy-start.1
  41.0 103.1 %all-gather.5.cloned.1.call-start = ((), (), s32[]{:S(2)}) async-start(), calls=%async_computation.7 | async-start | bytes 1179648 | tf_op jit(solution)/shard_map/all_gather | solution.py:49
  105.0 59.2 %all-reduce.5.cloned.1.call-start = ((), (), s32[]{:S(2)}) async-start(), calls=%async_computation.8 | async-start | bytes 524288 | tf_op jit(solution)/shard_map/psum | solution.py:50
  146.9 86.4 %reduce-scatter.7.cloned.1.call-start = ((), (), s32[]{:S(2)}) async-start(), calls=%async_computation.9 | async-start | bytes 1179648 | tf_op jit(solution)/shard_map/reduce_scatter | solution.py:46
  167.9 106.0 %all-gather.7.cloned.1.call-start = ((), (), s32[]{:S(2)}) async-start(), calls=%async_computation.10 | async-start | bytes 1179648 | tf_op jit(solution)/shard_map/all_gather | solution.py:49
  235.0 59.0 %all-reduce.7.cloned.1.call-start = ((), (), s32[]{:S(2)}) async-start(), calls=%async_computation.11 | async-start | bytes 524288 | tf_op jit(solution)/shard_map/psum | solution.py:50
  276.7 86.4 %reduce-scatter.9.cloned.1.call-start = ((), (), s32[]{:S(2)}) async-start(), calls=%async_computation.12 | async-start | bytes 1179648 | tf_op jit(solution)/shard_map/reduce_scatter | solution.py:46
  297.7 106.1 %all-gather.9.cloned.1.call-start = ((), (), s32[]{:S(2)}) async-start(), calls=%async_computation.13 | async-start | bytes 1179648 | tf_op jit(solution)/shard_map/all_gather | solution.py:49
  364.8 59.1 %all-reduce.9.cloned.1.call-start = ((), (), s32[]{:S(2)}) async-start(), calls=%async_computation.14 | async-start | bytes 524288 | tf_op jit(solution)/shard_map/psum | solution.py:50
  406.6 86.4 %reduce-scatter.11.cloned.1.call-start = ((), (), s32[]{:S(2)}) async-start(), calls=%async_computation.15 | async-start | bytes 1179648 | tf_op jit(solution)/shard_map/reduce_scatter | solution.py:46
  427.7 106.2 %all-gather.11.cloned.1.call-start = ((), (), s32[]{:S(2)}) async-start(), calls=%async_computation.16 | async-start | bytes 1179648 | tf_op jit(solution)/shard_map/all_gather | solution.py:49
  494.8 59.1 %all-reduce.11.cloned.1.call-start = ((), (), s32[]{:S(2)}) async-start(), calls=%async_computation.17 | async-start | bytes 524288 | tf_op jit(solution)/shard_map/psum | solution.py:50
  555.5 13.2 %all-to-all-start.1 = ((bf16[8,32,256]{2,1,0:T(8,128)(2,1)}), bf16[8,32,256]{2,1,0:T(8,128)(2,1)S(1)}, u32[]{:S(2)}, u32[]{:S(2)}) async-start(bf16[8,32,256]{2,1,0:T(8,128)(2,1)} %bitcast.27), calls=%async_computation.5 | async-start | bytes 262144 | tf_op jit(solution)/shard_map/all_to_all | solution.py:78
Sparse Core Ops, SparseCore 0:
  41.2 62.0 reduce-scatter.4
  105.5 38.5 all-gather.4
  147.0 17.1 all-reduce.4
  168.0 65.1 reduce-scatter.6
  235.3 38.5 all-gather.6
  276.8 17.1 all-reduce.6
  297.8 65.1 reduce-scatter.8
  365.3 38.5 all-gather.8
  406.7 17.1 all-reduce.8
  427.8 65.1 reduce-scatter.10
  495.3 38.5 all-gather.10
  536.7 17.1 all-reduce.10
where the time goes:
time: 577 us; the launch traced here: 576 us
  waiting for transfers between devices  407 us (71%)
  blocking collectives  101 us (18%)
  matrix products  27.1 us (5%)
  other arithmetic  15 us (3%)
  between operations  13.7 us (2%)
  starting transfers between devices  7.53 us (1%)
    reduce_scatter x4, waiting for transfers between devices, apply_layer(): summed = lax.psum_scatter(partial, 'seq', scatter_dimension=1, tiled=True)  174 us
    all_gather x4, waiting for transfers between devices, apply_layer(): hidden = lax.all_gather(hidden, 'seq', axis=1, tiled=True)  156 us
    psum x4, blocking collectives, apply_layer(): squares = lax.psum(jnp.sum(values * values, axis=1, keepdims=True), 'seq')  83.7 us
    psum x4, waiting for transfers between devices, apply_layer(): added = lax.psum(project_down(hidden, down_rows), 'mdl')  69.1 us
    all_to_all x1, blocking collectives, body(): state = lax.all_to_all(rows, 'seq', split_axis=1, concat_axis=0, tiled=True)  15.4 us
  transfers between devices with their start and end apart: 14, of which 13 were waited for; matrix products, arithmetic and copies ran while one was open for 1% of the time, Pallas kernels for 0%

commit v1 on v0

--- a/solution.py
+++ b/solution.py
@@ -6,6 +6,17 @@
 
 HOP = 128
 EPSILON = 1e-06
+
+
+def split_up(x, dim, count):
+    before, after = (x.shape[:dim], x.shape[dim + 1 :])
+    return jnp.moveaxis(x.reshape(*before, count, -1, *after), dim, 0)
+
+
+def laid_out(blocks, dim):
+    shape = list(blocks.shape[1:])
+    shape[dim] *= blocks.shape[0]
+    return jnp.moveaxis(blocks, 0, dim).reshape(shape)
 
 
 def shifted(x, axis, by):
@@ -75,7 +86,14 @@
     width = rows.shape[1]
     for layer in range(up_weight.shape[0]):
         state = apply_layer(state, up_weight[layer], down_weight[layer], width)
-    rows = lax.all_to_all(state, "seq", split_axis=0, concat_axis=1, tiled=True)
+    devices, index = (lax.axis_size("seq"), lax.axis_index("seq"))
+    parts = split_up(state, 0, devices)
+    outs = [parts[index]]
+    for step in range(1, devices):
+        sent = parts[index ^ step]
+        outs.append(lax.ppermute(sent, "seq", [(i_2, i_2 ^ step) for i_2 in range(devices)]))
+    parts = jnp.stack(outs)[index ^ jnp.arange(devices)]
+    rows = laid_out(parts, 1)
     full_rows = rows.reshape(streams, frames, width)
     half_streams = streams // lax.axis_size("mdl")
     return lax.dynamic_slice_in_dim(

time: 577 us -> 581 us (level)
    ppermute x0 -> x7, starting transfers between devices: none -> 11.2 us  [body(): lax.ppermute(sent, 'seq', [(i_2, i_2 ^ step) for i_2 in range(devices)])]
    all_to_all x1 -> x0, waiting for transfers between devices: 7.45 us -> none  [body(): rows = lax.all_to_all(state, 'seq', split_axis=0, concat_axis=1, tiled=True)]
    ppermute x0 -> x7, waiting for transfers between devices: none -> 6.18 us  [body(): lax.ppermute(sent, 'seq', [(i_2, i_2 ^ step) for i_2 in range(devices)])]
  transfers between devices with their start and end apart: 14 -> 20, of which waited for: 13 -> 15; matrix products, arithmetic and copies ran while one was open for 1% -> 1% of each run, Pallas kernels for 0% -> 0%
where the time goes in v1:
time: 581 us; the launch traced here: 580 us
  waiting for transfers between devices  405 us (70%)
  blocking collectives  101 us (17%)
  matrix products  26.9 us (5%)
  other arithmetic  14.3 us (2%)
  between operations  13.8 us (2%)
  starting transfers between devices  13 us (2%)
    reduce_scatter x4, waiting for transfers between devices, apply_layer(): summed = lax.psum_scatter(partial, 'seq', scatter_dimension=1, tiled=True)  174 us
    all_gather x4, waiting for transfers between devices, apply_layer(): hidden = lax.all_gather(hidden, 'seq', axis=1, tiled=True)  156 us
    psum x4, blocking collectives, apply_layer(): squares = lax.psum(jnp.sum(values * values, axis=1, keepdims=True), 'seq')  83.7 us
    psum x4, waiting for transfers between devices, apply_layer(): added = lax.psum(project_down(hidden, down_rows), 'mdl')  69 us
    all_to_all x1, blocking collectives, body(): state = lax.all_to_all(rows, 'seq', split_axis=1, concat_axis=0, tiled=True)  15.4 us
  transfers between devices with their start and end apart: 20, of which 15 were waited for; matrix products, arithmetic and copies ran while one was open for 1% of the time, Pallas kernels for 0%

profile of v1, /device:TPU:0, one launch (start us, length us, event | category | flops | bytes accessed | tf_op | source)
XLA Modules:
  0.0 580.3 jit_solution(3273580903190977727)
XLA Ops:
  9.5 4.7 convolution_bitcast_fusion
  14.3 1.9 copy-done.1
  17.1 1.9 slice_add_fusion
  20.9 2.0 all_gather.15
  22.9 15.4 %all_to_all.19 = bf16[32,8,256]{2,0,1:T(8,128)(2,1)S(1)} all-to-all(bf16[32,8,256]{2,0,1:T(8,128)(2,1)S(1)} %bitcast.117), channel_id=1, replica_groups=mesh['grp'=2,'seq'=8,'mdl'=2] {'seq'}, dimensions={1} | all-to-all | bytes 262144 | tf_op jit(solution)/shard_map/all_to_all | solution.py:85
  38.4 2.6 convolution_convert_fusion.3
  41.3 18.6 %psum.56 = f32[256,1]{0,1:T(1,128)S(1)} all-reduce(f32[256,1]{0,1:T(1,128)S(1)} %broadcast_in_dim.37), channel_id=1, replica_groups=mesh['grp'=2,'seq'=8,'mdl'=2] {'seq'}, use_global_device_ids=true, to_apply=%region_2.3 | all-reduce | flops 256 | bytes 2048 | tf_op jit(solution)/shard_map/psum | solution.py:55
  59.9 43.3 %reduce-scatter.5.cloned.1.call-done = bf16[256,256]{1,0:T(8,128)(2,1)} async-done(((bf16[256,2048]{1,0:T(8,128)(2,1)}), bf16[256,256]{1,0:T(8,128)(2,1)}) %reduce-scatter.5.cloned.1.call-update) | async-done | bytes 131088 | tf_op jit(solution)/shard_map/reduce_scatter | solution.py:57
  105.0 39.1 %all-gather.5.cloned.1.call-done = bf16[256,2048]{1,0:T(8,128)(2,1)} async-done(((bf16[256,256]{1,0:T(8,128)(2,1)}), bf16[256,2048]{1,0:T(8,128)(2,1)}) %all-gather.5.cloned.1.call-update) | async-done | bytes 1048592 | tf_op jit(solution)/shard_map/all_gather | solution.py:60
  144.0 2.7 fusion.14
  146.8 17.3 %all-reduce.5.cloned.1.call-done = f32[256,256]{1,0:T(8,128)} async-done(((f32[256,256]{1,0:T(8,128)}), f32[256,256]{1,0:T(8,128)}) %all-reduce.5.cloned.1.call-update) | async-done | bytes 262160 | tf_op jit(solution)/shard_map/psum | solution.py:61
  165.1 2.6 convolution_convert_fusion.2
  167.8 21.7 %psum.58 = f32[256,1]{0,1:T(1,128)S(1)} all-reduce(f32[256,1]{0,1:T(1,128)S(1)} %bitcast.119), channel_id=1, replica_groups=mesh['grp'=2,'seq'=8,'mdl'=2] {'seq'}, use_global_device_ids=true, to_apply=%region_6.7 | all-reduce | flops 256 | bytes 2048 | tf_op jit(solution)/shard_map/psum | solution.py:55
  189.5 43.6 %reduce-scatter.7.cloned.1.call-done = bf16[256,256]{1,0:T(8,128)(2,1)} async-done(((bf16[256,2048]{1,0:T(8,128)(2,1)}), bf16[256,256]{1,0:T(8,128)(2,1)}) %reduce-scatter.7.cloned.1.call-update) | async-done | bytes 131088 | tf_op jit(solution)/shard_map/reduce_scatter | solution.py:57
  234.9 38.8 %all-gather.7.cloned.1.call-done = bf16[256,2048]{1,0:T(8,128)(2,1)} async-done(((bf16[256,256]{1,0:T(8,128)(2,1)}), bf16[256,2048]{1,0:T(8,128)(2,1)}) %all-gather.7.cloned.1.call-update) | async-done | bytes 1048592 | tf_op jit(solution)/shard_map/all_gather | solution.py:60
  273.8 2.7 fusion.11
  276.6 17.3 %all-reduce.7.cloned.1.call-done = f32[256,256]{1,0:T(8,128)} async-done(((f32[256,256]{1,0:T(8,128)}), f32[256,256]{1,0:T(8,128)}) %all-reduce.7.cloned.1.call-update) | async-done | bytes 262160 | tf_op jit(solution)/shard_map/psum | solution.py:61
  294.9 2.6 convolution_convert_fusion.1
  297.6 21.7 %psum.60 = f32[256,1]{0,1:T(1,128)S(1)} all-reduce(f32[256,1]{0,1:T(1,128)S(1)} %bitcast.120), channel_id=1, replica_groups=mesh['grp'=2,'seq'=8,'mdl'=2] {'seq'}, use_global_device_ids=true, to_apply=%region_10.11 | all-reduce | flops 256 | bytes 2048 | tf_op jit(solution)/shard_map/psum | solution.py:55
  319.3 43.6 %reduce-scatter.9.cloned.1.call-done = bf16[256,256]{1,0:T(8,128)(2,1)} async-done(((bf16[256,2048]{1,0:T(8,128)(2,1)}), bf16[256,256]{1,0:T(8,128)(2,1)}) %reduce-scatter.9.cloned.1.call-update) | async-done | bytes 131088 | tf_op jit(solution)/shard_map/reduce_scatter | solution.py:57
  364.7 39.0 %all-gather.9.cloned.1.call-done = bf16[256,2048]{1,0:T(8,128)(2,1)} async-done(((bf16[256,256]{1,0:T(8,128)(2,1)}), bf16[256,2048]{1,0:T(8,128)(2,1)}) %all-gather.9.cloned.1.call-update) | async-done | bytes 1048592 | tf_op jit(solution)/shard_map/all_gather | solution.py:60
  403.7 2.7 fusion.8
  406.5 17.3 %all-reduce.9.cloned.1.call-done = f32[256,256]{1,0:T(8,128)} async-done(((f32[256,256]{1,0:T(8,128)}), f32[256,256]{1,0:T(8,128)}) %all-reduce.9.cloned.1.call-update) | async-done | bytes 262160 | tf_op jit(solution)/shard_map/psum | solution.py:61
  424.8 2.6 convolution_convert_fusion
  427.5 21.7 %psum.62 = f32[256,1]{0,1:T(1,128)S(1)} all-reduce(f32[256,1]{0,1:T(1,128)S(1)} %bitcast.121), channel_id=1, replica_groups=mesh['grp'=2,'seq'=8,'mdl'=2] {'seq'}, use_global_device_ids=true, to_apply=%region_14.15 | all-reduce | flops 256 | bytes 2048 | tf_op jit(solution)/shard_map/psum | solution.py:55
  449.2 43.6 %reduce-scatter.11.cloned.1.call-done = bf16[256,256]{1,0:T(8,128)(2,1)} async-done(((bf16[256,2048]{1,0:T(8,128)(2,1)}), bf16[256,256]{1,0:T(8,128)(2,1)}) %reduce-scatter.11.cloned.1.call-update) | async-done | bytes 131088 | tf_op jit(solution)/shard_map/reduce_scatter | solution.py:57
  494.6 39.0 %all-gather.11.cloned.1.call-done = bf16[256,2048]{1,0:T(8,128)(2,1)} async-done(((bf16[256,256]{1,0:T(8,128)(2,1)}), bf16[256,2048]{1,0:T(8,128)(2,1)}) %all-gather.11.cloned.1.call-update) | async-done | bytes 1048592 | tf_op jit(solution)/shard_map/all_gather | solution.py:60
  533.6 2.7 fusion.5
  536.4 17.2 %all-reduce.11.cloned.1.call-done = f32[256,256]{1,0:T(8,128)} async-done(((f32[256,256]{1,0:T(8,128)}), f32[256,256]{1,0:T(8,128)}) %all-reduce.11.cloned.1.call-update) | async-done | bytes 262160 | tf_op jit(solution)/shard_map/psum | solution.py:61
  558.2 2.7 collective-permute-start.4
  562.3 3.3 collective-permute-start.6
  567.8 4.2 collective-permute-done.7
  (89 shorter events, 26.2 us)
Async XLA Ops:
  6.5 12.9 %copy-start = (bf16[64,128,16]{1,2,0:T(8,128)(2,1)S(1)}, bf16[64,128,16]{1,2,0:T(8,128)(2,1)}, u32[]{:S(2)}) copy-start(bf16[64,128,16]{1,2,0:T(8,128)(2,1)} %param.7) | copy-start | bytes 786436
  6.5 96.6 %reduce-scatter.5.cloned.1.call-start = ((), (), s32[]{:S(2)}) async-start(), calls=%async_computation.5 | async-start | bytes 1179648 | tf_op jit(solution)/shard_map/reduce_scatter | solution.py:57
  7.5 9.2 %collective-permute-start = (f32[4,64,128]{2,1,0:T(8,128)S(1)}, f32[4,64,128]{2,1,0:T(8,128)S(1)}, u32[]{:S(2)}, u32[]{:S(2)}) collective-permute-start(f32[4,64,128]{2,1,0:T(8,128)S(1)} %slice.49), channel_id=1, source_target_pairs={{2,0},{4,2},{6,4},{8,6},{10,8},{12,10},{14,12},{3,1},{5,3},{7,5},{... | collective-permute-start | bytes 393224 | tf_op jit(solution)/shard_map/ppermute | solution.py:25
  9.5 7.0 %copy-start.2 = (s32[4]{0:T(128)S(1)}, s32[4]{0:T(128)}, u32[]{:S(2)}) copy-start(s32[4]{0:T(128)} %param.6) | copy-start | bytes 52
  14.3 1.9 copy-start.1
  41.0 103.0 %all-gather.5.cloned.1.call-start = ((), (), s32[]{:S(2)}) async-start(), calls=%async_computation.6 | async-start | bytes 1179648 | tf_op jit(solution)/shard_map/all_gather | solution.py:60
  104.9 59.2 %all-reduce.5.cloned.1.call-start = ((), (), s32[]{:S(2)}) async-start(), calls=%async_computation.7 | async-start | bytes 524288 | tf_op jit(solution)/shard_map/psum | solution.py:61
  146.8 86.4 %reduce-scatter.7.cloned.1.call-start = ((), (), s32[]{:S(2)}) async-start(), calls=%async_computation.8 | async-start | bytes 1179648 | tf_op jit(solution)/shard_map/reduce_scatter | solution.py:57
  167.8 106.0 %all-gather.7.cloned.1.call-start = ((), (), s32[]{:S(2)}) async-start(), calls=%async_computation.9 | async-start | bytes 1179648 | tf_op jit(solution)/shard_map/all_gather | solution.py:60
  234.9 58.9 %all-reduce.7.cloned.1.call-start = ((), (), s32[]{:S(2)}) async-start(), calls=%async_computation.10 | async-start | bytes 524288 | tf_op jit(solution)/shard_map/psum | solution.py:61
  276.5 86.4 %reduce-scatter.9.cloned.1.call-start = ((), (), s32[]{:S(2)}) async-start(), calls=%async_computation.11 | async-start | bytes 1179648 | tf_op jit(solution)/shard_map/reduce_scatter | solution.py:57
  297.5 106.1 %all-gather.9.cloned.1.call-start = ((), (), s32[]{:S(2)}) async-start(), calls=%async_computation.12 | async-start | bytes 1179648 | tf_op jit(solution)/shard_map/all_gather | solution.py:60
  364.6 59.1 %all-reduce.9.cloned.1.call-start = ((), (), s32[]{:S(2)}) async-start(), calls=%async_computation.13 | async-start | bytes 524288 | tf_op jit(solution)/shard_map/psum | solution.py:61
  406.4 86.4 %reduce-scatter.11.cloned.1.call-start = ((), (), s32[]{:S(2)}) async-start(), calls=%async_computation.14 | async-start | bytes 1179648 | tf_op jit(solution)/shard_map/reduce_scatter | solution.py:57
  427.4 106.1 %all-gather.11.cloned.1.call-start = ((), (), s32[]{:S(2)}) async-start(), calls=%async_computation.15 | async-start | bytes 1179648 | tf_op jit(solution)/shard_map/all_gather | solution.py:60
  494.5 59.1 %all-reduce.11.cloned.1.call-start = ((), (), s32[]{:S(2)}) async-start(), calls=%async_computation.16 | async-start | bytes 524288 | tf_op jit(solution)/shard_map/psum | solution.py:61
  554.6 7.7 %collective-permute-start.1 = (bf16[32,256]{1,0:T(8,128)(2,1)S(1)}, bf16[32,256]{1,0:T(8,128)(2,1)S(1)}, u32[]{:S(2)}, u32[]{:S(2)}) collective-permute-start(bf16[32,256]{1,0:T(8,128)(2,1)S(1)} %get-tuple-element.19), channel_id=1, source_target_pairs={{0,2},{2,0},{4,6},{6,4},{8,10},{10,8},{12,14},{14,12},{1,3},{3,1},... | collective-permute-start | bytes 49160 | tf_op jit(solution)/shard_map/ppermute | solution.py:94
  556.4 9.2 %collective-permute-start.2 = (bf16[32,256]{1,0:T(8,128)(2,1)S(1)}, bf16[32,256]{1,0:T(8,128)(2,1)S(1)}, u32[]{:S(2)}, u32[]{:S(2)}) collective-permute-start(bf16[32,256]{1,0:T(8,128)(2,1)S(1)} %get-tuple-element.18), channel_id=1, source_target_pairs={{0,4},{2,6},{4,0},{6,2},{8,12},{10,14},{12,8},{14,10},{1,5},{3,7},... | collective-permute-start | bytes 49160 | tf_op jit(solution)/shard_map/ppermute | solution.py:94
  557.9 7.9 %collective-permute-start.3 = (bf16[32,256]{1,0:T(8,128)(2,1)S(1)}, bf16[32,256]{1,0:T(8,128)(2,1)S(1)}, u32[]{:S(2)}, u32[]{:S(2)}) collective-permute-start(bf16[32,256]{1,0:T(8,128)(2,1)S(1)} %get-tuple-element.17), channel_id=1, source_target_pairs={{0,6},{2,4},{4,2},{6,0},{8,14},{10,12},{12,10},{14,8},{1,7},{3,5},... | collective-permute-start | bytes 49160 | tf_op jit(solution)/shard_map/ppermute | solution.py:94
  558.2 7.7 %collective-permute-start.4 = (bf16[32,256]{1,0:T(8,128)(2,1)S(1)}, bf16[32,256]{1,0:T(8,128)(2,1)S(1)}, u32[]{:S(2)}, u32[]{:S(2)}) collective-permute-start(bf16[32,256]{1,0:T(8,128)(2,1)S(1)} %get-tuple-element.16), channel_id=1, source_target_pairs={{0,8},{2,10},{4,12},{6,14},{8,0},{10,2},{12,4},{14,6},{1,9},{3,11}... | collective-permute-start | bytes 49160 | tf_op jit(solution)/shard_map/ppermute | solution.py:94
  560.9 5.5 collective-permute-start.5
  562.3 5.5 collective-permute-start.6
  565.6 6.4 %collective-permute-start.7 = (bf16[32,256]{1,0:T(8,128)(2,1)S(1)}, bf16[32,256]{1,0:T(8,128)(2,1)S(1)}, u32[]{:S(2)}, u32[]{:S(2)}) collective-permute-start(bf16[32,256]{1,0:T(8,128)(2,1)S(1)} %get-tuple-element.13), channel_id=1, source_target_pairs={{0,14},{2,12},{4,10},{6,8},{8,6},{10,4},{12,2},{14,0},{1,15},{3,13... | collective-permute-start | bytes 49160 | tf_op jit(solution)/shard_map/ppermute | solution.py:94
Sparse Core Ops, SparseCore 0:
  41.2 61.9 reduce-scatter.4
  105.4 38.5 all-gather.4
  146.9 17.1 all-reduce.4
  167.9 65.1 reduce-scatter.6
  235.2 38.5 all-gather.6
  276.6 17.1 all-reduce.6
  297.7 65.1 reduce-scatter.8
  365.1 38.5 all-gather.8
  406.5 17.1 all-reduce.8
  427.6 65.1 reduce-scatter.10
  495.0 38.5 all-gather.10
  536.4 17.1 all-reduce.10
